TPU v7x, 32 devices: a whole 2x2x4 slice. The times are simulated.
32 devices in a mesh: seq: 8 (over z, x), tp: 4 (over y, core).
Axes of the slice: x: 2, y: 2, z: 4, core: 2. Of those that a mesh axis runs over, the one named last changes fastest.
Arguments:
- hidden_in: bfloat16 [4, 24, 3072], P(None, None, 'seq'), may hold values from -30 to 30
- attn_gain: bfloat16 [3072], P('seq'), may hold values from 0.5 to 1.5
- w_query: bfloat16 [3072, 3072], P('seq', 'tp'), may hold values from -0.109375 to 0.109375
- w_key: bfloat16 [3072, 3072], P('seq', 'tp'), may hold values from -0.109375 to 0.109375
- w_value: bfloat16 [3072, 3072], P('seq', 'tp'), may hold values from -0.109375 to 0.109375
- w_out: bfloat16 [3072, 3072], P('tp', 'seq'), may hold values from -0.109375 to 0.109375
- mlp_gain: bfloat16 [3072], P('seq'), may hold values from 0.5 to 1.5
- w_gate: bfloat16 [3072, 8192], P('seq', 'tp'), may hold values from -0.109375 to 0.109375
- w_up: bfloat16 [3072, 8192], P('seq', 'tp'), may hold values from -0.109375 to 0.109375
- w_down: bfloat16 [8192, 3072], P('tp', 'seq'), may hold values from -0.0625 to 0.0625
- kv_pages: bfloat16 [2, 1664, 32, 3072], P(None, 'seq', None, 'tp'), may hold values from -260 to 260
- lengths: int32 [24], replicated, may hold values from 512 to 2044, as said below
- group_ids: int32 [24], replicated, may hold values from 0 to 1, as said below
- shared_table: int32 [2, 16], replicated, may hold values from 0 to 207, as said below
- own_table: int32 [24, 64], P(None, 'seq'), may hold values from 0 to 207, as said below
Outputs:
- hidden_out: bfloat16 [4, 24, 3072], P(None, None, 'seq')
- new_cache: bfloat16 [2, 4, 24, 3072], P(None, None, None, 'tp')
Inputs may be any that keep to these rules, and one draw needn't show every extreme that they name: `lengths`: one request in every draw has the length 2044. `group_ids`: each group number is named by exactly 12 requests. Entries are pages of the pool of the index of seq that holds the page's positions (prompt page p lies on index p // 8); on one index the pages named by shared_table and own_table are all different. `own_table`: entries are pages of the pool of the index of seq that holds the page's positions; entries of logical pages under 16 are never read.
All inputs are finite; a program needn't handle non-finite values.
Results may differ from a plain program's by a relative error of at most 0.0085.
The roundings to bfloat16 on the way count: a program that leaves them out, or rounds other values in their place, can miss the bound.
Values may be sent and summed in bfloat16 or wider, within the bound.
A program may use at most 192 MiB of HBM per device.

v0:
```python
import math
import jax
import jax.numpy as jnp
from jax import lax
from jax.sharding import PartitionSpec as P

D = 3072
HEAD_DIM = 96
SINKS = 4
WINDOW = 1024
EPSILON = 1e-05
ROPE_BASE = 10000.0
NEGATIVE = -1e30


def rotate(vector, position):
    halfway = vector.shape[-1] // 2
    frequency = ROPE_BASE ** (-(jnp.arange(halfway, dtype=jnp.float32) * 2.0 / vector.shape[-1]))
    angles = position[..., None].astype(jnp.float32) * frequency
    cosine = jnp.cos(angles)
    sine_part = jnp.sin(angles)
    first_half = vector[..., :halfway]
    second_half = vector[..., halfway:]
    return jnp.concatenate(
        [
            first_half * cosine - second_half * sine_part,
            second_half * cosine + first_half * sine_part,
        ],
        -1,
    )


def seq_total(partial_value, squares):
    return lax.psum((partial_value, squares), "seq")


def head_total(partial_value):
    return lax.psum(partial_value, "tp")


def body(
    hidden_in,
    attn_gain,
    w_query,
    w_key,
    w_value,
    w_out,
    mlp_gain,
    w_gate,
    w_up,
    w_down,
    kv_pages,
    lengths,
    group_ids,
    shared_table,
    own_table,
):
    seq_index = lax.axis_index("seq")
    step_count = hidden_in.shape[0]
    requests = hidden_in.shape[1]
    local_width = hidden_in.shape[2]
    head_cols = w_query.shape[1]
    local_heads = head_cols // HEAD_DIM
    unit_cols = w_gate.shape[1]
    page_rows = kv_pages.shape[2]
    local_pages = own_table.shape[1]
    block_len = local_pages * page_rows
    group_count = shared_table.shape[0]
    prompt_pages = shared_table.shape[1]
    score_scale = 1.0 / math.sqrt(HEAD_DIM)
    flat_rows = step_count * requests
    logical = seq_index * local_pages + jnp.arange(local_pages, dtype=jnp.int32)
    group_pick = (group_ids[:, None] == jnp.arange(group_count, dtype=jnp.int32)[None, :]).astype(
        jnp.int32
    )
    group_rows = jnp.sum(group_pick[:, :, None] * shared_table[None, :, :], axis=1)
    column_pick = (logical[:, None] == jnp.arange(prompt_pages, dtype=jnp.int32)[None, :]).astype(
        jnp.int32
    )
    shared_local = jnp.sum(group_rows[:, None, :] * column_pick[None, :, :], axis=2)
    physical = jnp.where(logical[None, :] < prompt_pages, shared_local, own_table)
    gathered = kv_pages[:, physical]
    cached_keys = gathered[0].reshape(requests, block_len, local_heads, HEAD_DIM)
    cached_values = (
        gathered[1].reshape(requests, block_len, local_heads, HEAD_DIM).astype(jnp.float32)
    )
    positions = seq_index * block_len + jnp.arange(block_len, dtype=jnp.int32)
    step_ids = jnp.arange(step_count, dtype=jnp.int32)
    owner_new = jnp.transpose((lengths[None, :] + step_ids[:, None]) // block_len == seq_index)
    attn_scale = attn_gain.astype(jnp.float32)
    mlp_scale = mlp_gain.astype(jnp.float32)
    w_pair = jnp.concatenate([w_gate, w_up], axis=1)
    residual = hidden_in.astype(jnp.float32).reshape(flat_rows, local_width)
    normed = (residual * attn_scale).astype(jnp.bfloat16)
    squares = jnp.sum(residual * residual, axis=-1)
    where_now = lengths[None, :] + step_ids[:, None]
    w_qkv = jnp.concatenate([w_query, w_key, w_value], axis=1)
    partial_value = jnp.dot(normed, w_qkv, preferred_element_type=jnp.float32)
    summed, square_sum = seq_total(partial_value, squares)
    inv_rms = lax.rsqrt(square_sum / D + EPSILON)
    projected = (summed * inv_rms[:, None]).reshape(step_count, requests, 3, local_heads, HEAD_DIM)
    queries = rotate(projected[:, :, 0], where_now[:, :, None]).astype(jnp.bfloat16)
    key_new = (
        rotate(projected[:, :, 1], where_now[:, :, None])
        .astype(jnp.bfloat16)
        .reshape(step_count, requests, head_cols)
    )
    value_new = projected[:, :, 2].astype(jnp.bfloat16).reshape(step_count, requests, head_cols)
    store_keys = key_new.reshape(step_count, requests, local_heads, HEAD_DIM)
    store_values = value_new.reshape(step_count, requests, local_heads, HEAD_DIM).astype(
        jnp.float32
    )
    in_window = positions[None, None, :] > lengths[None, :, None] + step_ids[:, None, None] - WINDOW
    is_live = (positions[None, None, :] < lengths[None, :, None]) & (
        (positions[None, None, :] < SINKS) | in_window
    )
    new_live = (step_ids[None, None, :] <= step_ids[:, None, None]) & owner_new[None, :, :]
    scores = (
        jnp.einsum("tbhd,bkhd->tbhk", queries, cached_keys, preferred_element_type=jnp.float32)
        * score_scale
    )
    new_scores = (
        jnp.einsum("tbhd,sbhd->tbhs", queries, store_keys, preferred_element_type=jnp.float32)
        * score_scale
    )
    scores = jnp.where(is_live[:, :, None, :], scores, NEGATIVE)
    new_scores = jnp.where(new_live[:, :, None, :], new_scores, NEGATIVE)
    local_peak = jnp.maximum(jnp.max(scores, axis=-1), jnp.max(new_scores, axis=-1))
    score_peak = lax.pmax(local_peak, "seq")
    weights = jnp.where(is_live[:, :, None, :], jnp.exp(scores - score_peak[..., None]), 0.0)
    new_weights = jnp.where(
        new_live[:, :, None, :], jnp.exp(new_scores - score_peak[..., None]), 0.0
    )
    weight_sum = jnp.sum(weights, axis=-1) + jnp.sum(new_weights, axis=-1)
    weighted = jnp.einsum("tbhk,bkhd->tbhd", weights, cached_values) + jnp.einsum(
        "tbhs,sbhd->tbhd", new_weights, store_values
    )
    local_sum = weight_sum
    local_weighted = weighted
    weight_sum, weighted = lax.psum((local_sum, local_weighted), "seq")
    attn = (weighted / weight_sum[..., None]).astype(jnp.bfloat16).reshape(flat_rows, head_cols)
    mid_rows = residual + head_total(jnp.dot(attn, w_out, preferred_element_type=jnp.float32))
    mlp_in = (mid_rows * mlp_scale).astype(jnp.bfloat16)
    mid_squares = jnp.sum(mid_rows * mid_rows, axis=-1)
    gate_up = jnp.dot(mlp_in, w_pair, preferred_element_type=jnp.float32)
    pair_sum, mid_sum = seq_total(gate_up, mid_squares)
    inv_mid = lax.rsqrt(mid_sum / D + EPSILON)[:, None]
    activated = (
        jax.nn.silu(pair_sum[:, :unit_cols] * inv_mid) * (pair_sum[:, unit_cols:] * inv_mid)
    ).astype(jnp.bfloat16)
    result = (
        mid_rows + head_total(jnp.dot(activated, w_down, preferred_element_type=jnp.float32))
    ).astype(jnp.bfloat16)
    hidden_out = result.reshape(step_count, requests, local_width)
    return (hidden_out, jnp.stack([key_new, value_new]))


def solution(mesh):
    return jax.shard_map(
        body,
        mesh=mesh,
        in_specs=(
            P(None, None, "seq"),
            P("seq"),
            P("seq", "tp"),
            P("seq", "tp"),
            P("seq", "tp"),
            P("tp", "seq"),
            P("seq"),
            P("seq", "tp"),
            P("seq", "tp"),
            P("tp", "seq"),
            P(None, "seq", None, "tp"),
            P(),
            P(),
            P(),
            P(None, "seq"),
        ),
        out_specs=(P(None, None, "seq"), P(None, None, None, "tp")),
        check_vma=False,
    )
```

profile of v0, /device:TPU:0, one launch (start us, length us, event | category | flops | bytes accessed | tf_op | source)
XLA Modules:
  0.0 413.2 jit_solution(18278633913271878751)
XLA Ops:
  7.3 0.8 convert_element_type.82
  8.1 0.9 fusion.40
  9.0 2.8 fusion.8
  11.8 0.1 fusion.39
  12.1 0.1 multiply_reduce_fusion.2
  12.2 0.1 multiply_reduce_fusion.1
  12.3 0.1 copy.33
  12.4 0.1 reshape.251
  12.5 17.1 %gather_fusion = bf16[192,2,32,768]{3,2,1,0:T(8,128)(2,1)} fusion(bf16[2,208,32,768]{3,2,1,0:T(8,128)(2,1)} %param.25, s32[1024]{0:T(1024)S(1)} %pad_clamp_fusion), kind=kCustom, calls=%fused_computation | custom fusion | bytes 37749504 | tf_op jit(solution)/shard_map/gather | solution.py:82
  29.7 9.6 %copy.69 = bf16[24,8,2,32,768]{4,3,1,0,2:T(8,128)(2,1)S(1)} copy(bf16[24,8,2,32,768]{4,3,2,1,0:T(8,128)(2,1)} %bitcast.48) | data formatting | bytes 37748736 | tf_op jit(solution)/shard_map/gather | solution.py:82
  39.2 6.9 %fusion.55 = (bf16[1,24,8,32,768]{4,3,2,1,0:T(8,128)(2,1)}, bf16[1,24,8,32,768]{4,3,2,1,0:T(8,128)(2,1)}) fusion(bf16[2,24,8,32,768]{4,3,2,1,0:T(8,128)(2,1)S(1)} %bitcast.47), kind=kLoop, calls=%fused_computation.100 | loop fusion | bytes 37748736 | tf_op jit(solution)/shard_map/slice | solution.py:83
  46.1 21.8 %reshape_squeeze.6 = bf16[24,256,8,96]{3,2,1,0:T(8,128)(2,1)} reshape(bf16[1,24,8,32,768]{4,3,2,1,0:T(8,128)(2,1)} %get-tuple-element.3) | data formatting | bytes 18874368 | tf_op jit(solution)/shard_map/reshape;squeeze | solution.py:85
  67.9 0.1 reduce_sum.59
  68.0 23.8 %psum.57 = f32[96]{0:T(128)S(1)} all-reduce(f32[96]{0:T(128)S(1)} %reduce_sum.59), channel_id=1, replica_groups=mesh['seq'=8,'tp'=4] {'seq'}, use_global_device_ids=true, to_apply=%region_4.5 | all-reduce | flops 96 | bytes 768 | tf_op jit(solution)/shard_map/psum | solution.py:34
  91.8 21.8 %reshape_squeeze.7 = bf16[24,256,8,96]{3,2,1,0:T(8,128)(2,1)} reshape(bf16[1,24,8,32,768]{4,3,2,1,0:T(8,128)(2,1)} %get-tuple-element.2) | data formatting | bytes 18874368 | tf_op jit(solution)/shard_map/reshape;squeeze | solution.py:83
  113.5 0.1 fusion.43
  113.7 0.1 broadcast_and_fusion
  113.9 0.1 or_and_fusion
  114.0 0.4 multiply_cosine_fusion
  114.4 2.3 broadcast_multiply_fusion
  116.7 2.0 reshape.246
  118.8 0.5 copy_bitcast_fusion.1
  119.3 0.4 subtract_convert_fusion
  119.7 0.4 multiply_subtract_fusion
  120.1 0.3 maximum_convert_fusion
  120.4 8.1 %fusion.57 = (f32[4,24,8]{0,2,1:T(8,128)S(1)}, f32[4,24,8,256]{3,0,2,1:T(4,128)S(1)}) fusion(bf16[4,24,8,48]{3,0,2,1:T(4,128)(2,1)S(1)} %get-tuple-element.9, bf16[4,24,8,48]{3,0,2,1:T(4,128)(2,1)S(1)} %get-tuple-element.8, bf16[24,256,8,96]{3,2,1,0:T(8,128)(2,1)} %reshape_squeeze.7, pred[4,24,256]{2,0,1:T(4,128)(4,1)S(1)} %or_and_fusion), kind=kOutput, calls=%fused_computation.102 | convolution fusion | flops 38632704 | bytes 10398720 | tf_op jit(solution)/shard_map/tbhd,bkhd->tbhk/dot_general | solution.py:119
  128.5 1.6 fusion.58
  130.2 33.8 %pmax.7 = f32[4,24,8]{0,2,1:T(8,128)S(1)} all-reduce(f32[4,24,8]{0,2,1:T(8,128)S(1)} %max.5), channel_id=1, replica_groups=mesh['seq'=8,'tp'=4] {'seq'}, use_global_device_ids=true, to_apply=%region_7.8 | all-reduce | flops 768 | bytes 6144 | tf_op jit(solution)/shard_map/pmax | solution.py:129
  164.0 7.2 %fusion = f32[24,8,96,4]{2,3,1,0:T(4,128)} fusion(bf16[24,256,8,96]{3,2,1,0:T(8,128)(2,1)} %reshape_squeeze.6, f32[4,24,8,256]{3,0,2,1:T(4,128)S(1)} %get-tuple-element.17, f32[4,24,8]{0,2,1:T(8,128)S(1)} %pmax.7, pred[4,24,256]{2,0,1:T(4,128)(4,1)S(1)} %or_and_fusion), kind=kOutput, calls=%fused_computation.2 | convolution fusion | flops 38141952 | bytes 10546176 | tf_op jit(solution)/shard_map/tbhk,bkhd->tbhd/dot_general | solution.py:135
  171.1 2.3 fusion.21
  173.5 0.4 fusion.34
  173.9 0.6 fusion.28
  174.5 36.2 %psum.59 = f32[4,24,8]{0,2,1:T(8,128)S(1)} all-reduce(f32[4,24,8]{0,2,1:T(8,128)S(1)} %add.156), channel_id=1, replica_groups=mesh['seq'=8,'tp'=4] {'seq'}, use_global_device_ids=true, to_apply=%region_11.12 | all-reduce | flops 768 | bytes 6144 | tf_op jit(solution)/shard_map/psum | solution.py:140
  210.7 33.2 %all-reduce.8.cloned.1.call-done = f32[4,24,8,96]{3,0,2,1:T(4,128)} async-done(((f32[4,24,8,96]{3,0,2,1:T(4,128)}), f32[4,24,8,96]{3,0,2,1:T(4,128)}) %all-reduce.8.cloned.1.call-update) | async-done | bytes 294928 | tf_op jit(solution)/shard_map/psum | solution.py:140
  243.9 1.3 divide_convert_fusion
  245.2 0.2 reshape.247
  245.4 2.0 fusion.59
  247.5 29.9 %all-reduce.10.cloned.1.call-done = f32[96,384]{1,0:T(8,128)} async-done(((f32[96,384]{1,0:T(8,128)}), f32[96,384]{1,0:T(8,128)}) %all-reduce.10.cloned.1.call-update) | async-done | bytes 147472 | tf_op jit(solution)/shard_map/psum | solution.py:38
  277.4 1.0 multiply_reduce_fusion
  278.4 3.8 fusion.4
  282.2 0.2 convert_element_type.94
  282.5 0.2 convert_element_type.93
  282.6 22.1 %psum.62 = f32[96]{0:T(128)S(1)} all-reduce(f32[96]{0:T(128)S(1)} %get-tuple-element.10), channel_id=1, replica_groups=mesh['seq'=8,'tp'=4] {'seq'}, use_global_device_ids=true, to_apply=%region_15.16 | all-reduce | flops 96 | bytes 768 | tf_op jit(solution)/shard_map/psum | solution.py:34
  304.8 67.5 %all-reduce.12.cloned.1.call-done = f32[96,4096]{1,0:T(8,128)} async-done(((f32[96,4096]{1,0:T(8,128)}), f32[96,4096]{1,0:T(8,128)}) %all-reduce.12.cloned.1.call-update) | async-done | bytes 1572880 | tf_op jit(solution)/shard_map/psum | solution.py:34
  372.3 2.5 fusion.32
  374.8 0.7 pad_maximum_fusion
  375.6 29.5 %all-reduce.14.cloned.1.call-done = f32[96,384]{1,0:T(8,128)} async-done(((f32[96,384]{1,0:T(8,128)}), f32[96,384]{1,0:T(8,128)}) %all-reduce.14.cloned.1.call-update) | async-done | bytes 147472 | tf_op jit(solution)/shard_map/psum | solution.py:38
  405.1 1.6 add_convert_fusion.1
  (52 shorter events, 1.0 us)
Async XLA Ops:
  7.2 365.1 %copy-start = (bf16[2048,384]{1,0:T(8,128)(2,1)S(1)}, bf16[2048,384]{1,0:T(8,128)(2,1)}, u32[]{:S(2)}) copy-start(bf16[2048,384]{1,0:T(8,128)(2,1)} %param.24) | copy-start | bytes 4718596
  7.2 4.7 %copy-start.1 = (bf16[4,24,384]{2,1,0:T(8,128)(2,1)S(1)}, bf16[4,24,384]{2,1,0:T(8,128)(2,1)}, u32[]{:S(2)}) copy-start(bf16[4,24,384]{2,1,0:T(8,128)(2,1)} %param.15) | copy-start | bytes 221188
  7.2 4.9 %copy-start.9 = (s32[24]{0:T(128)S(1)}, s32[24]{0:T(128)}, u32[]{:S(2)}) copy-start(s32[24]{0:T(128)} %param.27) | copy-start | bytes 292
  7.2 4.9 %copy-start.7 = (s32[2,16]{1,0:T(2,128)S(1)}, s32[2,16]{1,0:T(2,128)}, u32[]{:S(2)}) copy-start(s32[2,16]{1,0:T(2,128)} %param.28) | copy-start | bytes 388
  7.2 5.0 %copy-start.6 = (s32[24,8]{0,1:T(8,128)S(1)}, s32[24,8]{0,1:T(8,128)}, u32[]{:S(2)}) copy-start(s32[24,8]{0,1:T(8,128)} %param.29) | copy-start | bytes 2308
  7.2 107.2 %all-reduce.6.cloned.1.call-start = ((), (), s32[]{:S(2)}) async-start(), calls=%async_computation | async-start | bytes 1769472 | tf_op jit(solution)/shard_map/psum | solution.py:34
  11.7 232.2 %all-reduce.8.cloned.1.call-start = ((), (), s32[]{:S(2)}) async-start(), calls=%async_computation.1 | async-start | bytes 786432 | tf_op jit(solution)/shard_map/psum | solution.py:140
  91.8 21.8 %copy-start.5 = (s32[24]{0:T(128)S(1)}, s32[24]{0:T(128)}, u32[]{:S(2)}) copy-start(s32[24]{0:T(128)} %param.26) | copy-start | bytes 292
  119.7 0.7 copy-start.3
  119.7 0.7 copy-start.4
  171.1 76.4 %copy-start.8 = (bf16[384]{0:T(512)(128)(2,1)S(1)}, bf16[384]{0:T(512)(128)(2,1)}, u32[]{:S(2)}) copy-start(bf16[384]{0:T(512)(128)(2,1)} %param.21) | copy-start | bytes 2308
  173.4 104.0 %all-reduce.10.cloned.1.call-start = ((), (), s32[]{:S(2)}) async-start(), calls=%async_computation.2 | async-start | bytes 294912 | tf_op jit(solution)/shard_map/psum | solution.py:38
  247.4 124.9 %all-reduce.12.cloned.1.call-start = ((), (), s32[]{:S(2)}) async-start(), calls=%async_computation.3 | async-start | bytes 3145728 | tf_op jit(solution)/shard_map/psum | solution.py:34
  282.2 122.9 %all-reduce.14.cloned.1.call-start = ((), (), s32[]{:S(2)}) async-start(), calls=%async_computation.4 | async-start | bytes 294912 | tf_op jit(solution)/shard_map/psum | solution.py:38
  282.4 122.7 %copy-start.2 = (f32[96,384]{1,0:T(8,128)S(1)}, f32[96,384]{1,0:T(8,128)}, u32[]{:S(2)}) copy-start(f32[96,384]{1,0:T(8,128)} %all-reduce.10.cloned.1.call-done) | copy-start | bytes 442372
Sparse Core Ops, SparseCore 0:
  11.9 78.9 all-reduce.5
  173.5 70.3 all-reduce.7
  247.5 29.7 all-reduce.9
  282.3 89.9 all-reduce.11
  374.9 30.1 all-reduce.13
where the time goes:
time: 415 us; the launch traced here: 413 us
  waiting for transfers between devices  160 us (39%)
  blocking collectives  116 us (28%)
  local copies, waits for them, and re-layouts  80.6 us (19%)
  matrix products  30.1 us (7%)
  between operations  14.1 us (3%)
  other arithmetic  11.9 us (3%)
    psum x2, waiting for transfers between devices, seq_total(): return lax.psum((partial_value, squares), 'seq')  67.6 us
    psum x2, waiting for transfers between devices, head_total(): return lax.psum(partial_value, 'tp')  59.4 us
    psum x2, blocking collectives, seq_total(): return lax.psum((partial_value, squares), 'seq')  45.9 us
    psum x1, blocking collectives, body(): weight_sum, weighted = lax.psum((local_sum, local_weighted), 'seq')  36.2 us
    pmax x1, blocking collectives, body(): score_peak = lax.pmax(local_peak, 'seq')  33.8 us
    psum x1, waiting for transfers between devices, body(): weight_sum, weighted = lax.psum((local_sum, local_weighted), 'seq')  33.2 us
    gather x2, local copies, waits for them, and re-layouts, body(): gathered = kv_pages[:, physical]  26.7 us
    another operation x1, local copies, waits for them, and re-layouts, body(): gathered[1].reshape(requests, block_len, local_heads, HEAD_DIM)  21.8 us
  transfers between devices with their start and end apart: 5, of which 4 were waited for; matrix products, arithmetic and copies ran while one was open for 20% of the time, Pallas kernels for 0%

commit v1 on v0

--- a/solution.py
+++ b/solution.py
@@ -11,6 +11,11 @@
 EPSILON = 1e-05
 ROPE_BASE = 10000.0
 NEGATIVE = -1e30
+
+
+def gather_and_add(array, axis):
+    parts = lax.all_gather(array, axis)
+    return jnp.sum(parts, axis=0)
 
 
 def rotate(vector, position):
@@ -35,7 +40,7 @@
 
 
 def head_total(partial_value):
-    return lax.psum(partial_value, "tp")
+    return gather_and_add(partial_value, "tp")
 
 
 def body(

time: 415 us -> 362 us (0.87)
  waiting for transfers between devices: 160 us -> 98.6 us
  blocking collectives: 116 us -> 129 us
    psum x2 -> x0, waiting for transfers between devices: 59.4 us -> none  [head_total(): return lax.psum(partial_value, 'tp')]
    all_gather x0 -> x2, blocking collectives: none -> 15 us  [gather_and_add(): parts = lax.all_gather(array, axis)]
  transfers between devices with their start and end apart: 5 -> 3, of which waited for: 4 -> 2; matrix products, arithmetic and copies ran while one was open for 20% -> 23% of each run, Pallas kernels for 0% -> 0%
where the time goes in v1:
time: 362 us; the launch traced here: 360 us
  blocking collectives  129 us (36%)
  waiting for transfers between devices  98.6 us (27%)
  local copies, waits for them, and re-layouts  80.6 us (22%)
  matrix products  27 us (7%)
  between operations  14.1 us (4%)
  other arithmetic  11.2 us (3%)
    psum x2, waiting for transfers between devices, seq_total(): return lax.psum((partial_value, squares), 'seq')  66.2 us
    psum x2, blocking collectives, seq_total(): return lax.psum((partial_value, squares), 'seq')  44 us
    psum x1, blocking collectives, body(): weight_sum, weighted = lax.psum((local_sum, local_weighted), 'seq')  35.9 us
    pmax x1, blocking collectives, body(): score_peak = lax.pmax(local_peak, 'seq')  33.8 us
    psum x1, waiting for transfers between devices, body(): weight_sum, weighted = lax.psum((local_sum, local_weighted), 'seq')  32.3 us
    gather x2, local copies, waits for them, and re-layouts, body(): gathered = kv_pages[:, physical]  26.7 us
    another operation x1, local copies, waits for them, and re-layouts, body(): gathered[0].reshape(requests, block_len, local_heads, HEAD_DIM)  21.8 us
    another operation x1, local copies, waits for them, and re-layouts, body(): gathered[1].reshape(requests, block_len, local_heads, HEAD_DIM)  21.8 us
  transfers between devices with their start and end apart: 3, of which 2 were waited for; matrix products, arithmetic and copies ran while one was open for 23% of the time, Pallas kernels for 0%

profile of v1, /device:TPU:0, one launch (start us, length us, event | category | flops | bytes accessed | tf_op | source)
XLA Modules:
  0.0 360.4 jit_solution(15576846472849950109)
XLA Ops:
  7.3 0.8 convert_element_type.83
  8.1 0.9 fusion.40
  9.0 2.8 fusion.8
  11.8 0.1 fusion.39
  12.2 0.1 multiply_reduce_fusion.1
  12.3 0.1 copy.33
  12.4 0.1 reshape.252
  12.5 17.1 %gather_fusion = bf16[192,2,32,768]{3,2,1,0:T(8,128)(2,1)} fusion(bf16[2,208,32,768]{3,2,1,0:T(8,128)(2,1)} %param.25, s32[1024]{0:T(1024)S(1)} %pad_clamp_fusion), kind=kCustom, calls=%fused_computation | custom fusion | bytes 37749504 | tf_op jit(solution)/shard_map/gather | solution.py:87
  29.7 9.6 %copy.69 = bf16[24,8,2,32,768]{4,3,1,0,2:T(8,128)(2,1)S(1)} copy(bf16[24,8,2,32,768]{4,3,2,1,0:T(8,128)(2,1)} %bitcast.52) | data formatting | bytes 37748736 | tf_op jit(solution)/shard_map/gather | solution.py:87
  39.2 6.9 %fusion.56 = (bf16[1,24,8,32,768]{4,3,2,1,0:T(8,128)(2,1)}, bf16[1,24,8,32,768]{4,3,2,1,0:T(8,128)(2,1)}) fusion(bf16[2,24,8,32,768]{4,3,2,1,0:T(8,128)(2,1)S(1)} %bitcast.51), kind=kLoop, calls=%fused_computation.101 | loop fusion | bytes 37748736 | tf_op jit(solution)/shard_map/slice | solution.py:88
  46.1 21.8 %reshape_squeeze.6 = bf16[24,256,8,96]{3,2,1,0:T(8,128)(2,1)} reshape(bf16[1,24,8,32,768]{4,3,2,1,0:T(8,128)(2,1)} %get-tuple-element.3) | data formatting | bytes 18874368 | tf_op jit(solution)/shard_map/reshape;squeeze | solution.py:90
  67.9 0.1 reduce_sum.83
  68.0 23.8 %psum.43 = f32[96]{0:T(128)S(1)} all-reduce(f32[96]{0:T(128)S(1)} %reduce_sum.83), channel_id=1, replica_groups=mesh['seq'=8,'tp'=4] {'seq'}, use_global_device_ids=true, to_apply=%region_4.5 | all-reduce | flops 96 | bytes 768 | tf_op jit(solution)/shard_map/psum | solution.py:39
  91.8 21.8 %reshape_squeeze.7 = bf16[24,256,8,96]{3,2,1,0:T(8,128)(2,1)} reshape(bf16[1,24,8,32,768]{4,3,2,1,0:T(8,128)(2,1)} %get-tuple-element.2) | data formatting | bytes 18874368 | tf_op jit(solution)/shard_map/reshape;squeeze | solution.py:88
  113.5 0.1 fusion.44
  113.7 0.1 broadcast_and_fusion
  113.9 0.1 or_and_fusion
  114.0 0.4 multiply_cosine_fusion
  114.5 2.3 broadcast_multiply_fusion
  116.7 2.0 reshape.248
  118.8 0.5 copy_bitcast_fusion.1
  119.3 0.4 subtract_convert_fusion
  119.7 0.4 multiply_subtract_fusion
  120.1 0.3 maximum_convert_fusion
  120.3 9.0 %fusion.58 = (f32[4,24,8]{0,2,1:T(8,128)S(1)}, f32[4,24,8,256]{3,0,2,1:T(4,128)}) fusion(bf16[4,24,8,48]{3,0,2,1:T(4,128)(2,1)S(1)} %get-tuple-element.9, bf16[4,24,8,48]{3,0,2,1:T(4,128)(2,1)S(1)} %get-tuple-element.8, bf16[24,256,8,96]{3,2,1,0:T(8,128)(2,1)} %reshape_squeeze.7, pred[4,24,256]{2,0,1:T(4,128)(4,1)S(1)} %or_and_fusion), kind=kOutput, calls=%fused_computation.103 | convolution fusion | flops 38632704 | bytes 10398720 | tf_op jit(solution)/shard_map/tbhd,bkhd->tbhk/dot_general | solution.py:124
  129.3 0.6 fusion.59
  129.9 33.8 %pmax.7 = f32[4,24,8]{0,2,1:T(8,128)S(1)} all-reduce(f32[4,24,8]{0,2,1:T(8,128)S(1)} %max.5), channel_id=1, replica_groups=mesh['seq'=8,'tp'=4] {'seq'}, use_global_device_ids=true, to_apply=%region_7.8 | all-reduce | flops 768 | bytes 6144 | tf_op jit(solution)/shard_map/pmax | solution.py:134
  163.7 6.5 %fusion = f32[24,8,96,4]{2,3,1,0:T(4,128)S(1)} fusion(bf16[24,256,8,96]{3,2,1,0:T(8,128)(2,1)} %reshape_squeeze.6, f32[4,24,8,256]{3,0,2,1:T(4,128)} %get-tuple-element.15, f32[4,24,8]{0,2,1:T(8,128)S(1)} %pmax.7, pred[4,24,256]{2,0,1:T(4,128)(4,1)S(1)} %or_and_fusion), kind=kOutput, calls=%fused_computation.2 | convolution fusion | flops 38141952 | bytes 10546176 | tf_op jit(solution)/shard_map/tbhk,bkhd->tbhd/dot_general | solution.py:140
  170.2 1.2 fusion.21
  171.6 0.4 fusion.34
  172.0 1.7 fusion.28
  173.7 35.9 %psum.45 = f32[4,24,8]{0,2,1:T(8,128)S(1)} all-reduce(f32[4,24,8]{0,2,1:T(8,128)S(1)} %add.157), channel_id=1, replica_groups=mesh['seq'=8,'tp'=4] {'seq'}, use_global_device_ids=true, to_apply=%region_11.12 | all-reduce | flops 768 | bytes 6144 | tf_op jit(solution)/shard_map/psum | solution.py:145
  209.6 32.3 %all-reduce.6.cloned.1.call-done = f32[4,24,8,96]{3,0,2,1:T(4,128)} async-done(((f32[4,24,8,96]{3,0,2,1:T(4,128)}), f32[4,24,8,96]{3,0,2,1:T(4,128)}) %all-reduce.6.cloned.1.call-update) | async-done | bytes 294928 | tf_op jit(solution)/shard_map/psum | solution.py:145
  241.9 1.3 divide_convert_fusion
  243.2 0.2 reshape.249
  243.4 1.3 fusion.60
  244.7 7.5 %all-gather = f32[384,384]{1,0:T(8,128)S(1)} all-gather(f32[96,384]{1,0:T(8,128)S(1)} %fusion.60), channel_id=2, replica_groups=mesh['seq'=8,'tp'=4] {'tp'}, dimensions={0}, use_global_device_ids=true | all-gather | bytes 737280 | tf_op jit(solution)/shard_map/all_gather | solution.py:17
  252.3 3.8 %fusion.4 = f32[96,4096]{1,0:T(8,128)} fusion(bf16[96,384]{1,0:T(8,128)(2,1)S(1)} %fusion.42, bf16[384,2048]{1,0:T(8,128)(2,1)} %param.23, bf16[384,2048]{1,0:T(8,128)(2,1)} %param.22), kind=kOutput, calls=%fused_computation.6 | convolution fusion | flops 308281344 | bytes 4792320 | tf_op jit(solution)/shard_map/dot_general | solution.py:150
  256.1 0.2 convert_element_type.95
  256.3 0.2 convert_element_type.94
  256.5 0.7 pad_maximum_fusion
  257.2 0.1 multiply_reduce_fusion
  257.3 0.1 reduce_sum.89
  257.4 20.2 %psum.47 = f32[96]{0:T(128)S(1)} all-reduce(f32[96]{0:T(128)S(1)} %reduce_sum.89), channel_id=1, replica_groups=mesh['seq'=8,'tp'=4] {'seq'}, use_global_device_ids=true, to_apply=%region_15.16 | all-reduce | flops 96 | bytes 768 | tf_op jit(solution)/shard_map/psum | solution.py:39
  277.6 66.2 %all-reduce.8.cloned.1.call-done = f32[96,4096]{1,0:T(8,128)} async-done(((f32[96,4096]{1,0:T(8,128)}), f32[96,4096]{1,0:T(8,128)}) %all-reduce.8.cloned.1.call-update) | async-done | bytes 1572880 | tf_op jit(solution)/shard_map/psum | solution.py:39
  343.8 1.8 fusion.32
  345.6 7.5 %all-gather.1 = f32[384,384]{1,0:T(8,128)S(1)} all-gather(f32[96,384]{1,0:T(8,128)S(1)} %fusion.32), channel_id=3, replica_groups=mesh['seq'=8,'tp'=4] {'tp'}, dimensions={0}, use_global_device_ids=true | all-gather | bytes 737280 | tf_op jit(solution)/shard_map/all_gather | solution.py:17
  353.2 0.7 add_convert_fusion.1
  (46 shorter events, 0.9 us)
Async XLA Ops:
  7.2 336.6 %copy-start = (bf16[2048,384]{1,0:T(8,128)(2,1)S(1)}, bf16[2048,384]{1,0:T(8,128)(2,1)}, u32[]{:S(2)}) copy-start(bf16[2048,384]{1,0:T(8,128)(2,1)} %param.24) | copy-start | bytes 4718596
  7.2 4.7 %copy-start.1 = (bf16[4,24,384]{2,1,0:T(8,128)(2,1)S(1)}, bf16[4,24,384]{2,1,0:T(8,128)(2,1)}, u32[]{:S(2)}) copy-start(bf16[4,24,384]{2,1,0:T(8,128)(2,1)} %param.15) | copy-start | bytes 221188
  7.2 4.9 %copy-start.6 = (s32[24]{0:T(128)S(1)}, s32[24]{0:T(128)}, u32[]{:S(2)}) copy-start(s32[24]{0:T(128)} %param.27) | copy-start | bytes 292
  7.2 4.9 %copy-start.4 = (s32[2,16]{1,0:T(2,128)S(1)}, s32[2,16]{1,0:T(2,128)}, u32[]{:S(2)}) copy-start(s32[2,16]{1,0:T(2,128)} %param.28) | copy-start | bytes 388
  7.2 5.0 %copy-start.3 = (s32[24,8]{0,1:T(8,128)S(1)}, s32[24,8]{0,1:T(8,128)}, u32[]{:S(2)}) copy-start(s32[24,8]{0,1:T(8,128)} %param.29) | copy-start | bytes 2308
  7.2 107.2 %all-reduce.4.cloned.1.call-start = ((), (), s32[]{:S(2)}) async-start(), calls=%async_computation | async-start | bytes 1769472 | tf_op jit(solution)/shard_map/psum | solution.py:39
  11.7 230.2 %all-reduce.6.cloned.1.call-start = ((), (), s32[]{:S(2)}) async-start(), calls=%async_computation.1 | async-start | bytes 786432 | tf_op jit(solution)/shard_map/psum | solution.py:145
  91.8 21.8 %copy-start.2 = (s32[24]{0:T(128)S(1)}, s32[24]{0:T(128)}, u32[]{:S(2)}) copy-start(s32[24]{0:T(128)} %param.26) | copy-start | bytes 292
  91.8 21.9 %copy-start.5 = (bf16[384]{0:T(512)(128)(2,1)S(1)}, bf16[384]{0:T(512)(128)(2,1)}, u32[]{:S(2)}) copy-start(bf16[384]{0:T(512)(128)(2,1)} %param.21) | copy-start | bytes 2308
  171.5 172.3 %all-reduce.8.cloned.1.call-start = ((), (), s32[]{:S(2)}) async-start(), calls=%async_computation.2 | async-start | bytes 3145728 | tf_op jit(solution)/shard_map/psum | solution.py:39
Sparse Core Ops, SparseCore 0:
  11.9 78.9 all-reduce.3
  171.6 70.2 all-reduce.5
  256.2 87.5 all-reduce.7
